TPU v7x, 32 devices: a whole 2x2x4 slice. The times are simulated.
32 devices in a mesh: geom: 2 (over x), pair: 16 (over z, y, core).
Axes of the slice: x: 2, y: 2, z: 4, core: 2. Of those that a mesh axis runs over, the one named last changes fastest.
Arguments:
- walkers: float32 [32, 64, 512], P(('geom', 'pair')), parts along dimension 0, may hold values from -6 to 6
- cholesky: bfloat16 [10240, 256, 513], P('geom', 'pair'), parts along dimension 0, may hold values from -0.33663118 to 0.33663118
- field_seeds: int32 [5120, 32], P('pair', 'geom'), parts along dimension 1, may hold values from 0 to 131071
- slot_order: int32 [32], P('geom'), parts along dimension 0, may hold values from 0 to 15, each once
Outputs:
- moved: float32 [32, 64, 512], P(('geom', 'pair')), parts along dimension 0
- log_weights: float32 [32], P(('geom', 'pair')), parts along dimension 0
There are 2 independent parts, one for each index of `geom`. A program takes and returns all parts, laid end to end along the dimension named above; each array names one. Nothing has to cross between parts.
Inputs may be any that keep to these rules, and one draw needn't show every extreme that they name: `slot_order`: a permutation of the walker numbers.
All inputs are finite; a program needn't handle non-finite values.
Results may differ from a plain program's by a relative error of at most 0.0044.
Values may be sent and summed in bfloat16 or wider, within the bound.
A program may use at most 320 MiB of HBM per device.

v0:
```python
import math

import jax
import jax.numpy as jnp
from jax import lax
from jax.experimental import pallas as pl
from jax.experimental.pallas import tpu as pltpu
from jax.sharding import PartitionSpec as P

sqrt_step = 0.1
VMEM = pl.BlockSpec(memory_space=pltpu.VMEM)


def flip_matrix(size):
    row = lax.broadcasted_iota(jnp.int32, (size, size), 0)
    col = lax.broadcasted_iota(jnp.int32, (size, size), 1)
    return jnp.where(row + col == size - 1, 1.0, 0.0).astype(jnp.bfloat16)


def exact_dot(a, b):
    return jnp.dot(a, b, preferred_element_type=jnp.float32)


def fold_kernel(green_ref, out_ref):
    orbits = green_ref.shape[0]
    halfway = orbits // 2
    flip_half = flip_matrix(halfway)
    upper = exact_dot(flip_half, green_ref[:halfway, :])
    lower = exact_dot(green_ref[halfway:, :], flip_matrix(orbits))
    joined = jnp.concatenate([upper, lower], axis=1)
    rolled = pltpu.roll(joined, orbits + halfway + 1, 1, stride=1, stride_axis=0)
    column = lax.broadcasted_iota(jnp.int32, (halfway, 2 * orbits), 1)
    weighted = jnp.where((column == 0) | (column == orbits), rolled, 2.0 * rolled)
    ordered = exact_dot(flip_half, weighted.astype(jnp.bfloat16))
    out_ref[...] = ordered[:, : orbits + 1].astype(jnp.bfloat16)


def fold(green):
    orbits = green.shape[0]
    return pl.pallas_call(
        fold_kernel,
        out_shape=jax.ShapeDtypeStruct((orbits // 2, orbits + 1), jnp.bfloat16),
        in_specs=[VMEM],
        out_specs=VMEM,
        name="fold",
    )(green)


def propagate_kernel(packed_ref, orbital_ref, out_ref):
    halfway, width = packed_ref.shape
    orbits = width - 1
    packed = packed_ref[...].astype(jnp.float32)
    padded = jnp.concatenate(
        [packed, jnp.zeros((halfway, 2 * orbits - width), jnp.float32)], axis=1
    )
    spread = pltpu.roll(padded, 0, 1, stride=1, stride_axis=0)
    backward = spread[:, orbits:].astype(jnp.bfloat16)
    turned = exact_dot(flip_matrix(halfway), backward).astype(jnp.bfloat16)
    lower = exact_dot(turned, flip_matrix(orbits))
    upper = jnp.concatenate([spread[:, :orbits], lower], axis=0)
    row = lax.broadcasted_iota(jnp.int32, (orbits, orbits), 0)
    col = lax.broadcasted_iota(jnp.int32, (orbits, orbits), 1)
    potential = jnp.where(col >= row, upper, upper.T).astype(jnp.bfloat16)
    term = orbital_ref[...]
    count = term.shape[0]
    result = term
    for degree in range(1, 7):
        high = term.astype(jnp.bfloat16)
        rest = term - high.astype(jnp.float32)
        middle = rest.astype(jnp.bfloat16)
        low = (rest - middle.astype(jnp.float32)).astype(jnp.bfloat16)
        product = exact_dot(jnp.concatenate([high, middle, low], axis=0), potential)
        term = (
            product[2 * count :] + product[count : 2 * count] + product[:count]
        ) * (1.0 / degree)
        result = result + term
    out_ref[...] = result


def propagate(packed_potential, orbital_matrix):
    return pl.pallas_call(
        propagate_kernel,
        out_shape=jax.ShapeDtypeStruct(orbital_matrix.shape, jnp.float32),
        in_specs=[VMEM, VMEM],
        out_specs=VMEM,
        name="propagate",
    )(packed_potential, orbital_matrix)


def meet_everyone(devices, own):
    barrier = pltpu.get_barrier_semaphore()

    def greet(step, carry):
        peer = lax.rem(own + step, devices)
        pl.semaphore_signal(
            barrier, inc=1, device_id={"pair": peer}, device_id_type=pl.DeviceIdType.MESH
        )
        return carry

    lax.fori_loop(1, devices, greet, 0)
    pl.semaphore_wait(barrier, devices - 1)


def remote(source, target, send_sem, recv_sem, step, peer):
    return pltpu.make_async_remote_copy(
        src_ref=source,
        dst_ref=target,
        send_sem=send_sem.at[step],
        recv_sem=recv_sem.at[step],
        device_id={"pair": peer},
        device_id_type=pl.DeviceIdType.MESH,
    )


def exchange_kernel(devices, in_ref, out_ref, send_sem, recv_sem, local_sem):
    own = lax.axis_index("pair")
    local = pltpu.make_async_copy(in_ref.at[own], out_ref.at[own], local_sem)
    local.start()
    meet_everyone(devices, own)

    def start(step, carry):
        peer = lax.rem(own + step, devices)
        remote(in_ref.at[peer], out_ref.at[own], send_sem, recv_sem, step, peer).start()
        return carry

    def finish(step, carry):
        peer = lax.rem(own + step, devices)
        source = lax.rem(own + devices - step, devices)
        remote(in_ref.at[peer], out_ref.at[source], send_sem, recv_sem, step, peer).wait()
        return carry

    lax.fori_loop(1, devices, start, 0)
    lax.fori_loop(1, devices, finish, 0)
    local.wait()


def exchange(blocks, devices, collective_id, name):
    return pl.pallas_call(
        lambda *refs: exchange_kernel(devices, *refs),
        out_shape=jax.ShapeDtypeStruct(blocks.shape, blocks.dtype),
        in_specs=[VMEM],
        out_specs=VMEM,
        scratch_shapes=[
            pltpu.SemaphoreType.DMA((devices,)),
            pltpu.SemaphoreType.DMA((devices,)),
            pltpu.SemaphoreType.DMA,
        ],
        compiler_params=pltpu.CompilerParams(
            collective_id=collective_id, has_side_effects=True
        ),
        name=name,
    )(blocks)


def fields_kernel(
    devices, partial_ref, noise_ref, shifted_ref, log_ref,
    arrived, own_shifted, own_log, all_log,
    bias_send, bias_recv, field_send, field_recv, log_send, log_recv,
):
    own = lax.axis_index("pair")
    meet_everyone(devices, own)

    def bias_copy(step, slot):
        peer = lax.rem(own + step, devices)
        return remote(partial_ref.at[peer], arrived.at[slot], bias_send, bias_recv, step, peer)

    def field_copy(step, slot):
        peer = lax.rem(own + step, devices)
        return remote(own_shifted, shifted_ref.at[slot], field_send, field_recv, step, peer)

    def log_copy(step, slot):
        peer = lax.rem(own + step, devices)
        return remote(own_log, all_log.at[slot], log_send, log_recv, step, peer)

    def start_bias(step, carry):
        bias_copy(step, own).start()
        return carry

    def finish_bias(step, total):
        source = lax.rem(own + devices - step, devices)
        bias_copy(step, source).wait()
        return total + arrived[source]

    lax.fori_loop(1, devices, start_bias, 0)
    bias = sqrt_step * lax.fori_loop(1, devices, finish_bias, partial_ref[own])
    noise = noise_ref[...]
    shifted = (noise - bias).astype(jnp.bfloat16)
    own_shifted[...] = shifted
    terms = jnp.sum(noise * bias - 0.5 * bias * bias, axis=1, keepdims=True)
    terms = jnp.broadcast_to(terms, own_log.shape)
    own_log[...] = terms

    def start_fields(step, carry):
        field_copy(step, own).start()
        return carry

    def start_logs(step, carry):
        log_copy(step, own).start()
        return carry

    def finish_fields(step, carry):
        source = lax.rem(own + devices - step, devices)
        field_copy(step, source).wait()
        return carry

    def finish_logs(step, total):
        source = lax.rem(own + devices - step, devices)
        log_copy(step, source).wait()
        return total + all_log[source]

    lax.fori_loop(1, devices, start_fields, 0)
    lax.fori_loop(1, devices, start_logs, 0)
    shifted_ref[own] = shifted
    lax.fori_loop(1, devices, finish_fields, 0)
    log_ref[...] = lax.fori_loop(1, devices, finish_logs, terms)


def fields(partial_bias, noise, devices):
    walk_total, chol_local = noise.shape
    sems = pltpu.SemaphoreType.DMA((devices,))
    return pl.pallas_call(
        lambda *refs: fields_kernel(devices, *refs),
        out_shape=(
            jax.ShapeDtypeStruct((devices, walk_total, chol_local), jnp.bfloat16),
            jax.ShapeDtypeStruct((walk_total, 128), jnp.float32),
        ),
        in_specs=[VMEM, VMEM],
        out_specs=(VMEM, VMEM),
        scratch_shapes=[
            pltpu.VMEM((devices, walk_total, chol_local), jnp.float32),
            pltpu.VMEM((walk_total, chol_local), jnp.bfloat16),
            pltpu.VMEM((walk_total, 128), jnp.float32),
            pltpu.VMEM((devices, walk_total, 128), jnp.float32),
        ] + [sems] * 6,
        compiler_params=pltpu.CompilerParams(collective_id=1, has_side_effects=True),
        name="fields",
    )(partial_bias, noise)


def density(orbital_matrix):
    intersection = jnp.dot(orbital_matrix, orbital_matrix.T, precision=lax.Precision.HIGHEST)
    factor = jnp.linalg.cholesky(intersection)
    rotated = lax.linalg.triangular_solve(factor, orbital_matrix, left_side=True, lower=True)
    return jnp.dot(rotated.T, rotated, precision=lax.Precision.HIGHEST)


def gaussian(seed_values):
    first = (seed_values % 65521 * 7919 + 13) % 65521
    second = (seed_values // 2 * 3037 + 101) % 65521
    uniform_one = (first.astype(jnp.float32) + 0.5) / 65521.0
    uniform_two = (second.astype(jnp.float32) + 0.5) / 65521.0
    return jnp.sqrt(-2.0 * jnp.log(uniform_one)) * jnp.cos(2.0 * math.pi * uniform_two)


def per_device(walkers, cholesky, field_seeds, slot_order):
    walk_local = walkers.shape[0]
    orbits = walkers.shape[2]
    halfway = orbits // 2
    devices = lax.axis_size("pair")
    own_index = lax.axis_index("pair")
    chol_total = cholesky.shape[0]
    rows_local = cholesky.shape[1]
    row_width = cholesky.shape[2]
    chol_local = chol_total // devices
    walk_total = walk_local * devices
    noise = gaussian(field_seeds[:, slot_order]).T
    greens = jax.vmap(density)(walkers).astype(jnp.bfloat16)
    folded = jnp.stack([fold(greens[w]) for w in range(walk_local)], axis=0)
    blocks = folded.reshape(walk_local, devices, rows_local, row_width).swapaxes(0, 1)
    packed = exchange(blocks, devices, 0, "density_out").reshape(
        walk_total, rows_local, row_width
    )
    partial_bias = lax.dot_general(
        cholesky, packed, (((1, 2), (1, 2)), ((), ())), preferred_element_type=jnp.float32
    ).T
    partial_bias = partial_bias.reshape(walk_total, devices, chol_local).swapaxes(0, 1)
    all_shifted, log_total = fields(partial_bias, noise, devices)
    shifted = all_shifted.swapaxes(0, 1).reshape(walk_total, chol_total)
    potential = sqrt_step * lax.dot_general(
        shifted, cholesky, (((1,), (0,)), ((), ())), preferred_element_type=jnp.float32
    )
    outgoing = potential.astype(jnp.bfloat16).reshape(
        devices, walk_local, rows_local, row_width
    )
    returned = exchange(outgoing, devices, 2, "potential_back")
    own_potential = returned.swapaxes(0, 1).reshape(walk_local, halfway, row_width)
    moved = jnp.stack(
        [propagate(own_potential[w], walkers[w]) for w in range(walk_local)], axis=0
    )
    own_log = lax.dynamic_slice_in_dim(log_total[:, 0], own_index * walk_local, walk_local, 0)
    return (moved, own_log)


def solution(mesh):
    return jax.shard_map(
        per_device,
        mesh=mesh,
        in_specs=(
            P(("geom", "pair"), None, None),
            P("geom", "pair", None),
            P("pair", "geom"),
            P("geom"),
        ),
        out_specs=(P(("geom", "pair"), None, None), P(("geom", "pair"))),
        check_vma=False,
    )
```

profile of v0, /device:TPU:0, one launch (start us, length us, event | category | flops | bytes accessed | tf_op | source)
XLA Modules:
  0.0 384.1 jit_solution(12286738746239246031)
XLA Ops:
  0.6 0.0 copy-start
  0.6 1.2 fusion.35
  1.9 0.1 copy.13
  2.0 5.8 %custom-call.7 = f32[1,64,64]{2,1,0:T(8,128)S(1)} custom-call(f32[1,64,64]{2,1,0:T(8,128)S(1)} %fusion.12), custom_call_target="Cholesky" | custom-call | tf_op jit(solution)/shard_map/vmap(jit(cholesky))/cholesky | solution.py:242
  7.9 0.6 compare_reduce_fusion
  8.5 0.7 fusion.11
  9.2 4.9 %custom-call.8 = f32[1,1,64,64]{2,3,1,0:T(8,128)S(1)} custom-call(f32[1,1,64,64]{3,2,1,0:T(8,128)S(1)} %fusion.11), custom_call_target="InvertDiagBlocksLowerTriangular" | custom-call | tf_op jit(solution)/shard_map/vmap()/triangular_solve | solution.py:243
  14.1 1.2 fusion.13
  15.3 1.8 convolution_convert_fusion.green_ref
  17.1 2.5 fold.1
  19.6 13.9 %density_out.1 = bf16[16,1,16,513]{3,2,1,0:T(8,128)(2,1)} custom-call(bf16[16,1,16,513]{3,2,1,0:T(8,128)(2,1)} %bitcast.38), custom_call_target="tpu_custom_call" | custom-call | tf_op jit(solution)/shard_map/density_out/pallas_call | solution.py:138
  33.5 0.0 copy-start.2
  33.5 155.3 %dot_general.19 = bf16[16,320,16,513]{1,0,2,3:T(8,128)(2,1)} reshape(bf16[5120,16,513]{0,1,2:T(8,128)(2,1)} %param.5) | data formatting | bytes 168099840 | tf_op jit(solution)/shard_map/dot_general | solution.py:273
  188.8 85.2 %fusion.4.refs_0_ = f32[16,16,320]{2,1,0:T(8,128)} fusion(bf16[16,320,16,513]{1,0,2,3:T(8,128)(2,1)} %dot_general.19, bf16[16,16,513]{2,1,0:T(8,128)(2,1)S(1)} %bitcast.41), kind=kOutput, calls=%fused_computation.6 | convolution fusion | flops 1344798720 | bytes 84640256 | tf_op jit(solution)/shard_map/dot_general | solution.py:273
  274.1 0.6 gather_fusion
  274.7 0.8 fusion.24.refs_1_
  275.4 26.4 %fields.1 = (bf16[16,16,320]{2,1,0:T(8,128)(2,1)}, f32[16,128]{1,0:T(8,128)}) custom-call(f32[16,16,320]{2,1,0:T(8,128)} %fusion.4.refs_0_, f32[16,320]{1,0:T(8,128)} %fusion.24.refs_1_), custom_call_target="tpu_custom_call" | custom-call | tf_op jit(solution)/shard_map/fields/pallas_call | solution.py:221
  301.8 1.2 constant_dynamic-slice_fusion
  303.0 1.0 copy.16
  304.0 0.2 reshape.95
  304.2 63.4 %fusion.2 = f32[16,16,513]{2,0,1:T(8,128)S(1)} fusion(bf16[16,5120,1]{1,0,2:T(8,128)(2,1)S(1)} %reshape.95, bf16[5120,16,513]{0,1,2:T(8,128)(2,1)} %param.5), kind=kOutput, calls=%fused_computation.3 | convolution fusion | flops 1344798720 | bytes 84739072 | tf_op jit(solution)/shard_map/dot_general | solution.py:279
  367.6 1.0 fusion.8.refs_0_
  368.6 11.9 %potential_back.1 = bf16[16,1,16,513]{3,2,1,0:T(8,128)(2,1)} custom-call(bf16[16,1,16,513]{3,2,1,0:T(8,128)(2,1)} %fusion.8.refs_0_), custom_call_target="tpu_custom_call" | custom-call | tf_op jit(solution)/shard_map/potential_back/pallas_call | solution.py:138
  380.5 3.6 propagate.1
  (8 shorter events, 0.1 us)
Async XLA Ops:
  0.6 273.4 %copy-start = (s32[320,16]{0,1:T(8,128)S(1)}, s32[320,16]{0,1:T(8,128)}, u32[]{:S(2)}) copy-start(s32[320,16]{0,1:T(8,128)} %param.6) | copy-start | bytes 61444
  33.5 155.4 %copy-start.1 = (bf16[16,1,16,513]{3,2,1,0:T(8,128)(2,1)S(1)}, bf16[16,1,16,513]{3,2,1,0:T(8,128)(2,1)}, u32[]{:S(2)}) copy-start(bf16[16,1,16,513]{3,2,1,0:T(8,128)(2,1)} %density_out.1) | copy-start | bytes 787972
  33.5 240.6 %copy-start.2 = (s32[16]{0:T(128)S(1)}, s32[16]{0:T(128)}, u32[]{:S(2)}) copy-start(s32[16]{0:T(128)} %param.7) | copy-start | bytes 196
where the time goes:
time: 388 us; the launch traced here: 384 us
  local copies, waits for them, and re-layouts  158 us (41%)
  matrix products  153 us (39%)
  Pallas kernels  58.3 us (15%)
  other arithmetic  13.8 us (4%)
    dot_general x1, local copies, waits for them, and re-layouts, per_device(): lax.dot_general(cholesky, packed, (((1, 2), (1, 2)), ((), ())), preferred...  155 us
    dot_general x1, matrix products, per_device(): lax.dot_general(cholesky, packed, (((1, 2), (1, 2)), ((), ())), preferred...  85.2 us
    dot_general x1, matrix products, per_device(): lax.dot_general(shifted, cholesky, (((1,), (0,)), ((), ())), preferred_el...  63.4 us
    pallas_call x1, Pallas kernels, fields(): pl.pallas_call(lambda *refs: fields_kernel(devices, *refs), out_shape=(ja...  26.4 us
    pallas_call x2, Pallas kernels, exchange(): pl.pallas_call(lambda *refs: exchange_kernel(devices, *refs), out_shape=j...  25.7 us

commit v1 on v0

--- a/solution.py
+++ b/solution.py
@@ -170,7 +170,7 @@
 
     def log_copy(step, slot):
         peer = lax.rem(own + step, devices)
-        return remote(own_log, all_log.at[slot], log_send, log_recv, step, peer)
+        return remote(own_log.at[peer], all_log.at[slot], log_send, log_recv, step, peer)
 
     def start_bias(step, carry):
         bias_copy(step, own).start()
@@ -187,8 +187,7 @@
     shifted = (noise - bias).astype(jnp.bfloat16)
     own_shifted[...] = shifted
     terms = jnp.sum(noise * bias - 0.5 * bias * bias, axis=1, keepdims=True)
-    terms = jnp.broadcast_to(terms, own_log.shape)
-    own_log[...] = terms
+    own_log[...] = jnp.broadcast_to(terms[:, :, None].reshape(own_log.shape[:2] + (1,)), own_log.shape)
 
     def start_fields(step, carry):
         field_copy(step, own).start()
@@ -212,25 +211,26 @@
     lax.fori_loop(1, devices, start_logs, 0)
     shifted_ref[own] = shifted
     lax.fori_loop(1, devices, finish_fields, 0)
-    log_ref[...] = lax.fori_loop(1, devices, finish_logs, terms)
+    log_ref[...] = lax.fori_loop(1, devices, finish_logs, own_log[own])
 
 
 def fields(partial_bias, noise, devices):
     walk_total, chol_local = noise.shape
+    walk_local = walk_total // devices
     sems = pltpu.SemaphoreType.DMA((devices,))
     return pl.pallas_call(
         lambda *refs: fields_kernel(devices, *refs),
         out_shape=(
             jax.ShapeDtypeStruct((devices, walk_total, chol_local), jnp.bfloat16),
-            jax.ShapeDtypeStruct((walk_total, 128), jnp.float32),
+            jax.ShapeDtypeStruct((walk_local, 128), jnp.float32),
         ),
         in_specs=[VMEM, VMEM],
         out_specs=(VMEM, VMEM),
         scratch_shapes=[
             pltpu.VMEM((devices, walk_total, chol_local), jnp.float32),
             pltpu.VMEM((walk_total, chol_local), jnp.bfloat16),
-            pltpu.VMEM((walk_total, 128), jnp.float32),
-            pltpu.VMEM((devices, walk_total, 128), jnp.float32),
+            pltpu.VMEM((devices, walk_local, 128), jnp.float32),
+            pltpu.VMEM((devices, walk_local, 128), jnp.float32),
         ] + [sems] * 6,
         compiler_params=pltpu.CompilerParams(collective_id=1, has_side_effects=True),
         name="fields",
@@ -257,7 +257,6 @@
     orbits = walkers.shape[2]
     halfway = orbits // 2
     devices = lax.axis_size("pair")
-    own_index = lax.axis_index("pair")
     chol_total = cholesky.shape[0]
     rows_local = cholesky.shape[1]
     row_width = cholesky.shape[2]
@@ -270,25 +269,29 @@
     packed = exchange(blocks, devices, 0, "density_out").reshape(
         walk_total, rows_local, row_width
     )
-    partial_bias = lax.dot_general(
-        cholesky, packed, (((1, 2), (1, 2)), ((), ())), preferred_element_type=jnp.float32
-    ).T
+    flat_packed = packed.transpose(0, 2, 1).reshape(walk_total, row_width * rows_local)
+    flat_chol = cholesky.transpose(2, 1, 0).reshape(row_width * rows_local, chol_total)
+    partial_bias = lax.optimization_barrier(
+        jnp.dot(flat_packed, flat_chol, preferred_element_type=jnp.float32)
+    )
     partial_bias = partial_bias.reshape(walk_total, devices, chol_local).swapaxes(0, 1)
     all_shifted, log_total = fields(partial_bias, noise, devices)
     shifted = all_shifted.swapaxes(0, 1).reshape(walk_total, chol_total)
     potential = sqrt_step * lax.dot_general(
-        shifted, cholesky, (((1,), (0,)), ((), ())), preferred_element_type=jnp.float32
-    )
-    outgoing = potential.astype(jnp.bfloat16).reshape(
-        devices, walk_local, rows_local, row_width
+        shifted, flat_chol, (((1,), (1,)), ((), ())), preferred_element_type=jnp.float32
+    )
+    potential = lax.optimization_barrier(potential.astype(jnp.bfloat16))
+    outgoing = (
+        potential.reshape(walk_total, row_width, rows_local)
+        .transpose(0, 2, 1)
+        .reshape(devices, walk_local, rows_local, row_width)
     )
     returned = exchange(outgoing, devices, 2, "potential_back")
     own_potential = returned.swapaxes(0, 1).reshape(walk_local, halfway, row_width)
     moved = jnp.stack(
         [propagate(own_potential[w], walkers[w]) for w in range(walk_local)], axis=0
     )
-    own_log = lax.dynamic_slice_in_dim(log_total[:, 0], own_index * walk_local, walk_local, 0)
-    return (moved, own_log)
+    return (moved, log_total[:, 0])
 
 
 def solution(mesh):

time: 388 us -> 149 us (0.38)
  local copies, waits for them, and re-layouts: 158 us -> 8.63 us
  matrix products: 153 us -> 67.5 us
    dot_general x1 -> x0, local copies, waits for them, and re-layouts: 155 us -> none  [per_device(): lax.dot_general(cholesky, packed, (((1, 2), (1, 2)), ((), ())), preferred...]
    dot_general x2, matrix products: 149 us -> 63.2 us  [the longest x1 32.3 us: per_device(): lax.dot_general(shifted, flat_chol, (((1,), (1,)), ((), ())), preferred_e...]
    reshape x0 -> x4, local copies, waits for them, and re-layouts: none -> 4.14 us  [the longest x2 3.15 us: per_device(): potential.reshape(walk_total, row_width, rows_local).transpose(0, 2, 1)]
where the time goes in v1:
time: 149 us; the launch traced here: 147 us
  matrix products  67.5 us (45%)
  Pallas kernels  55.1 us (37%)
  other arithmetic  13.5 us (9%)
  local copies, waits for them, and re-layouts  8.63 us (6%)
  between operations  1.93 us (1%)
    dot_general x1, matrix products, per_device(): lax.dot_general(shifted, flat_chol, (((1,), (1,)), ((), ())), preferred_e...  32.3 us
    dot_general x1, matrix products, per_device(): jnp.dot(flat_packed, flat_chol, preferred_element_type=jnp.float32)  31 us
    pallas_call x1, Pallas kernels, fields(): pl.pallas_call(lambda *refs: fields_kernel(devices, *refs), out_shape=(ja...  26 us
    pallas_call x2, Pallas kernels, exchange(): pl.pallas_call(lambda *refs: exchange_kernel(devices, *refs), out_shape=j...  22.9 us
    another operation x3, other arithmetic, density(): factor = jnp.linalg.cholesky(intersection)  6.52 us
    another operation x2, other arithmetic, density(): lax.linalg.triangular_solve(factor, orbital_matrix, left_side=True, lower...  5.55 us
    pallas_call x1, Pallas kernels, propagate(): pl.pallas_call(propagate_kernel, out_shape=jax.ShapeDtypeStruct(orbital_m...  3.65 us
    reshape x2, local copies, waits for them, and re-layouts, per_device(): potential.reshape(walk_total, row_width, rows_local).transpose(0, 2, 1)  3.15 us

profile of v1, /device:TPU:0, one launch (start us, length us, event | category | flops | bytes accessed | tf_op | source)
XLA Modules:
  0.0 146.7 jit_solution(5543798163022820318)
XLA Ops:
  0.6 0.7 compare_select_fusion
  1.4 0.6 gather_fusion
  2.0 0.8 fusion.19.refs_1_
  2.7 1.2 fusion.30
  4.1 5.8 %custom-call.7 = f32[1,64,64]{2,1,0:T(8,128)S(1)} custom-call(f32[1,64,64]{2,1,0:T(8,128)S(1)} %fusion.7), custom_call_target="Cholesky" | custom-call | tf_op jit(solution)/shard_map/vmap(jit(cholesky))/cholesky | solution.py:242
  9.9 0.6 compare_reduce_fusion
  10.6 0.7 fusion.6
  11.2 4.9 %custom-call.8 = f32[1,1,64,64]{2,3,1,0:T(8,128)S(1)} custom-call(f32[1,1,64,64]{3,2,1,0:T(8,128)S(1)} %fusion.6), custom_call_target="InvertDiagBlocksLowerTriangular" | custom-call | tf_op jit(solution)/shard_map/vmap()/triangular_solve | solution.py:243
  16.1 1.2 fusion.8
  17.4 1.8 %convolution_convert_fusion.green_ref = bf16[512,512]{1,0:T(8,128)(2,1)} fusion(f32[64,512]{1,0:T(8,128)S(1)} %fusion.8), kind=kOutput, calls=%fused_computation.6 | convolution fusion | flops 201588736 | bytes 655360 | tf_op jit(solution)/shard_map/vmap()/dot_general | solution.py:244
  19.2 2.5 %fold.1 = bf16[256,513]{1,0:T(8,128)(2,1)} custom-call(bf16[512,512]{1,0:T(8,128)(2,1)} %convolution_convert_fusion.green_ref), custom_call_target="tpu_custom_call" | custom-call | tf_op jit(solution)/shard_map/fold/pallas_call | solution.py:40
  21.7 13.8 %density_out.1 = bf16[16,1,16,513]{3,2,1,0:T(8,128)(2,1)} custom-call(bf16[16,1,16,513]{3,2,1,0:T(8,128)(2,1)} %bitcast.48), custom_call_target="tpu_custom_call" | custom-call | tf_op jit(solution)/shard_map/density_out/pallas_call | solution.py:138
  35.5 2.6 %copy.18 = bf16[16,513,16]{2,0,1:T(8,128)(2,1)S(1)} copy(bf16[16,513,16]{1,2,0:T(8,128)(2,1)} %bitcast.46) | data formatting | bytes 525312 | tf_op jit(solution)/shard_map/transpose | solution.py:272
  38.2 31.0 %fusion.3 = f32[16,5120]{1,0:T(8,128)S(1)} fusion(bf16[16,513,16]{2,0,1:T(8,128)(2,1)S(1)} %copy.18, bf16[5120,16,513]{0,1,2:T(8,128)(2,1)} %param.5), kind=kOutput, calls=%fused_computation.5 | convolution fusion | flops 1344798720 | bytes 84640256 | tf_op jit(solution)/shard_map/dot_general | solution.py:275
  69.1 0.1 reshape.89
  69.3 0.9 copy.22
  70.1 26.0 %fields.1 = (bf16[16,16,320]{2,1,0:T(8,128)(2,1)}, f32[1,128]{1,0:T(1,128)}) custom-call(f32[16,16,320]{2,1,0:T(8,128)} %bitcast.45, f32[16,320]{1,0:T(8,128)} %fusion.19.refs_1_), custom_call_target="tpu_custom_call" | custom-call | tf_op jit(solution)/shard_map/fields/pallas_call | solution.py:221
  96.2 1.0 copy.15
  97.2 0.2 reshape.90
  97.3 32.3 %fusion.2 = bf16[16,8208]{1,0:T(8,128)(2,1)S(1)} fusion(bf16[16,5120]{1,0:T(8,128)(2,1)S(1)} %reshape.90, bf16[8208,5120]{1,0:T(8,128)(2,1)} %bitcast.12), kind=kOutput, calls=%fused_computation.4 | convolution fusion | flops 1345061376 | bytes 84476416 | tf_op jit(solution)/shard_map/dot_general | solution.py:280
  129.6 1.6 %reshape.92 = bf16[16,513,16]{2,1,0:T(8,128)(2,1)S(1)} reshape(bf16[16,8208]{1,0:T(8,128)(2,1)S(1)} %fusion.2) | data formatting | bytes 525312 | tf_op jit(solution)/shard_map/reshape | solution.py:285
  131.2 1.6 %copy.16 = bf16[16,513,16]{1,2,0:T(8,128)(2,1)} copy(bf16[16,513,16]{2,1,0:T(8,128)(2,1)S(1)} %reshape.92) | data formatting | bytes 525312 | tf_op jit(solution)/shard_map/reshape | solution.py:285
  132.8 9.1 %potential_back.1 = bf16[16,1,16,513]{3,2,1,0:T(8,128)(2,1)} custom-call(bf16[16,1,16,513]{3,2,1,0:T(8,128)(2,1)} %bitcast.47), custom_call_target="tpu_custom_call" | custom-call | tf_op jit(solution)/shard_map/potential_back/pallas_call | solution.py:138
  141.9 3.6 %propagate.1 = f32[64,512]{1,0:T(8,128)} custom-call(bf16[256,513]{1,0:T(8,128)(2,1)} %bitcast.49, f32[64,512]{1,0:T(8,128)} %bitcast.50), custom_call_target="tpu_custom_call" | custom-call | tf_op jit(solution)/shard_map/propagate/pallas_call | solution.py:81
  (8 shorter events, 0.2 us)
Async XLA Ops:
  0.6 0.7 copy-start
  96.2 49.3 %copy-start.1 = (f32[1,128]{1,0:T(1,128)S(1)}, f32[1,128]{1,0:T(1,128)}, u32[]{:S(2)}) copy-start(f32[1,128]{1,0:T(1,128)} %get-tuple-element.5) | copy-start | bytes 1540
